TPU v7x, 128 devices: a whole 4x4x4 slice. The times are simulated.
128 devices in a mesh: row: 8 (over x_hi, y), col: 16 (over x_lo, z, core).
Axes of the slice: x: 4 (x_hi: 2, x_lo: 2; x = x_hi * 2 + x_lo), y: 4, z: 4, core: 2. Of those that a mesh axis runs over, the one named last changes fastest.
Arguments:
- latent: bfloat16 [256, 81920], P('row', 'col'), may hold values from -6 to 6
- tile_reach: int32 [8, 16, 4], replicated, may hold values from 1 to 4
- first_weight: bfloat16 [3, 3, 320, 320], replicated, may hold values from -0.109375 to 0.109375
- first_bias: float32 [320], replicated, may hold values from -3 to 3
- second_weight: bfloat16 [3, 3, 320, 320], replicated, may hold values from -0.109375 to 0.109375
- second_bias: float32 [320], replicated, may hold values from -3 to 3
- proj_weight: bfloat16 [320, 512], replicated, may hold values from -0.3125 to 0.3125
- upper_weight: bfloat16 [3, 3, 512, 512], replicated, may hold values from -0.09375 to 0.09375
- upper_bias: float32 [512], replicated, may hold values from -3 to 3
- lower_weight: bfloat16 [3, 3, 512, 512], replicated, may hold values from -0.09375 to 0.09375
- lower_bias: float32 [512], replicated, may hold values from -3 to 3
Outputs:
- decoded: bfloat16 [512, 512, 512], P(('row', 'col'))
All inputs are finite; a program needn't handle non-finite values.
Results may differ from a plain program's by a relative error of at most 0.0065.
Values may be sent and summed in bfloat16 or wider, within the bound.
A program may use at most 64 MiB of HBM per device.

v0:
```python
import functools

import jax
import jax.numpy as jnp
from jax import lax
from jax.experimental import pallas as pl
from jax.experimental.pallas import tpu as pltpu
from jax.sharding import PartitionSpec as P

MARGIN = 4
SIDE = 8
PAD = 8
F32 = jnp.float32
BF = jnp.bfloat16
MESH = pl.DeviceIdType.MESH
VM = pl.BlockSpec(memory_space=pltpu.VMEM)
ANY = pl.BlockSpec(memory_space=pl.ANY)
SM = pl.BlockSpec(memory_space=pltpu.SMEM)
AROUND = [(dr, dc) for dr in (-1, 0, 1) for dc in (-1, 0, 1) if (dr, dc) != (0, 0)]


def peer(row, col, dr, dc):
    rows, cols = lax.axis_size("row"), lax.axis_size("col")
    return lax.rem(row + (dr + rows), rows), lax.rem(col + (dc + cols), cols)


def halo_kernel(core_ref, *refs):
    lands, (send, recv) = refs[:8], refs[8:]
    rows, cols = core_ref.shape[:2]
    row, col = lax.axis_index("row"), lax.axis_index("col")
    barrier = pltpu.get_barrier_semaphore()
    for dr, dc in AROUND:
        pl.semaphore_signal(barrier, inc=1, device_id=peer(row, col, dr, dc), device_id_type=MESH)
    pl.semaphore_wait(barrier, len(AROUND))
    copies = []
    for n, (dr, dc) in enumerate(AROUND):
        rs = {-1: pl.ds(rows - MARGIN, MARGIN), 0: pl.ds(0, rows), 1: pl.ds(0, MARGIN)}[dr]
        cs = {-1: pl.ds(cols - SIDE, SIDE), 0: pl.ds(0, cols), 1: pl.ds(0, SIDE)}[dc]
        copies.append(
            pltpu.make_async_remote_copy(
                src_ref=core_ref.at[rs, cs],
                dst_ref=lands[n],
                send_sem=send.at[n],
                recv_sem=recv.at[n],
                device_id=peer(row, col, -dr, -dc),
                device_id_type=MESH,
            )
        )
        copies[-1].start()
    for c in copies:
        c.wait()


def halo(core):
    rows, cols, ch = core.shape
    shapes = [
        jax.ShapeDtypeStruct((rows if dr == 0 else MARGIN, cols if dc == 0 else SIDE, ch), core.dtype)
        for dr, dc in AROUND
    ]
    lands = pl.pallas_call(
        halo_kernel,
        out_shape=shapes,
        in_specs=[VM],
        out_specs=[VM] * 8,
        scratch_shapes=[pltpu.SemaphoreType.DMA((8,)), pltpu.SemaphoreType.DMA((8,))],
        compiler_params=pltpu.CompilerParams(collective_id=0, has_side_effects=True),
        name="halo",
    )(core)
    got = dict(zip(AROUND, lands))
    got[0, 0] = core
    m = MARGIN
    bands = []
    for dr in (-1, 0, 1):
        bands.append(
            jnp.concatenate([got[dr, -1][:, SIDE - m :], got[dr, 0], got[dr, 1][:, :m]], axis=1)
        )
    return jnp.concatenate(bands, axis=0)


def blend_kernel(y_ref, count_ref, out_ref, *refs):
    lands, (can, send, recv, send2, recv2, self_sem) = refs[:8], refs[8:]
    rows, cols = count_ref.shape[:2]
    core = rows - 2
    row, col = lax.axis_index("row"), lax.axis_index("col")
    n_col = lax.axis_size("col")
    barrier = pltpu.get_barrier_semaphore()
    greet = [peer(row, col, 0, o) for o in range(1, n_col)]
    greet += [peer(row, col, dr, dc) for dr, dc in AROUND if dr != 0]
    for g in greet:
        pl.semaphore_signal(barrier, inc=1, device_id=g, device_id_type=MESH)
    pl.semaphore_wait(barrier, len(greet))
    m, edge = MARGIN, MARGIN + 1
    top = y_ref.shape[0]
    copies = []
    for n, (dr, dc) in enumerate(AROUND):
        rs = {-1: pl.ds(top - edge, edge), 0: pl.ds(m - 1, rows), 1: pl.ds(0, edge)}[dr]
        cs = {-1: pl.ds(SIDE + cols, SIDE), 0: pl.ds(SIDE, cols), 1: pl.ds(0, SIDE)}[dc]
        copies.append(
            pltpu.make_async_remote_copy(
                src_ref=y_ref.at[rs, cs],
                dst_ref=lands[n],
                send_sem=send.at[n],
                recv_sem=recv.at[n],
                device_id=peer(row, col, -dr, -dc),
                device_id_type=MESH,
            )
        )
        copies[-1].start()
    for c in copies:
        c.wait()
    got = dict(zip(AROUND, lands))

    def put(lo, num, middle):
        here = pl.ds(lo, num)
        total = y_ref[pl.ds(m - 1 + lo, num), SIDE : SIDE + cols].astype(F32)
        left = got[0, -1][here].astype(F32)
        right = got[0, 1][here].astype(F32)
        if not middle:
            dr = -1 if lo == 0 else 1
            total += got[dr, 0][...].astype(F32)
            left += got[dr, -1][...].astype(F32)
            right += got[dr, 1][...].astype(F32)
        total += jnp.concatenate([left, right], axis=1)
        n = count_ref[here]
        can[here] = jnp.where(n > 0, total / jnp.maximum(n, 1.0), 0.0).astype(BF)

    put(0, edge, False)
    put(edge, rows - 2 * edge, True)
    put(rows - edge, edge, False)
    mine = pl.ds(pl.multiple_of(cols * col, cols), cols)
    step = core // n_col
    deep = step + 2
    own = pltpu.make_async_copy(can.at[pl.ds(step * col, deep)], out_ref.at[:, mine], self_sem)
    own.start()
    copies = []
    for o in range(1, n_col):
        to = peer(row, col, 0, o)
        copies.append(
            pltpu.make_async_remote_copy(
                src_ref=can.at[pl.ds(step * to[1], deep)],
                dst_ref=out_ref.at[:, mine],
                send_sem=send2.at[o],
                recv_sem=recv2.at[o],
                device_id=to,
                device_id_type=MESH,
            )
        )
        copies[-1].start()
    own.wait()
    for o in range(1, n_col):
        copies[o - 1].wait_send()
        src = peer(row, col, 0, -o)
        pltpu.make_async_remote_copy(
            src_ref=can.at[pl.ds(0, deep)],
            dst_ref=out_ref.at[:, pl.ds(pl.multiple_of(cols * src[1], cols), cols)],
            send_sem=send2.at[o],
            recv_sem=recv2.at[o],
            device_id=src,
            device_id_type=MESH,
        ).wait_recv()


def blend(y, count):
    rows, cols = count.shape[:2]
    ch = y.shape[2]
    n_col = lax.axis_size("col")
    shapes = [
        pltpu.VMEM((rows if dr == 0 else MARGIN + 1, cols if dc == 0 else SIDE, ch), BF) for dr, dc in AROUND
    ]
    deep = (rows - 2) // n_col + 2
    return pl.pallas_call(
        blend_kernel,
        out_shape=jax.ShapeDtypeStruct((deep, n_col * cols, ch), BF),
        in_specs=[VM, VM],
        out_specs=VM,
        scratch_shapes=shapes
        + [
            pltpu.VMEM((rows, cols, ch), BF),
            pltpu.SemaphoreType.DMA((8,)),
            pltpu.SemaphoreType.DMA((8,)),
            pltpu.SemaphoreType.DMA((n_col,)),
            pltpu.SemaphoreType.DMA((n_col,)),
            pltpu.SemaphoreType.DMA,
        ],
        compiler_params=pltpu.CompilerParams(collective_id=1, has_side_effects=True),
        name="blend",
    )(y, count)


def spread(g):
    outer = 0.5 * (g[0] + g[2])
    mid = 0.5 * g[1]
    return [g[0], outer + mid, outer - mid, g[2]]


def weights_kernel(up_ref, lo_ref, uo_ref, lo_out_ref):
    rows, d = up_ref.shape[2:]

    def chunk(n, _):
        sl = pl.ds(pl.multiple_of(n * 16, 16), 16)
        for lane in range(0, d, 128):
            ln = slice(lane, lane + 128)
            cols = []
            for b in range(3):
                w = [up_ref[a, b, sl, ln].astype(F32) for a in range(3)]
                cols.append([w[0], w[0] + w[1] + w[2], w[2]])
            for p in range(3):
                v = [cols[0][p], cols[0][p] + cols[1][p] + cols[2][p], cols[2][p]]
                for q in range(3):
                    uo_ref[3 * p + q, sl, ln] = v[q].astype(BF)
            cols = [spread([lo_ref[a, b, sl, ln].astype(F32) for a in range(3)]) for b in range(3)]
            for r in range(4):
                v = spread([cols[b][r] for b in range(3)])
                for c in range(4):
                    lo_out_ref[4 * r + c, sl, ln] = v[c].astype(BF)
        return 0

    lax.fori_loop(0, rows // 16, chunk, 0)


def transform_weights(upper, lower):
    d = upper.shape[2]
    step = 64
    return pl.pallas_call(
        weights_kernel,
        grid=(d // step,),
        in_specs=[pl.BlockSpec((3, 3, step, d), lambda i: (0, 0, i, 0))] * 2,
        out_specs=[pl.BlockSpec((9, step, d), lambda i: (0, i, 0)), pl.BlockSpec((16, step, d), lambda i: (0, i, 0))],
        out_shape=[jax.ShapeDtypeStruct((9, d, d), BF), jax.ShapeDtypeStruct((16, d, d), BF)],
        compiler_params=pltpu.CompilerParams(vmem_limit_bytes=48 * 2**20),
        cost_estimate=pl.CostEstimate(flops=20 * 9 * d * d, bytes_accessed=2 * (18 + 25) * d * d, transcendentals=0),
        name="weights",
    )(upper, lower)


def dot(a, b):
    return jnp.dot(a, b, preferred_element_type=F32)


def decode_kernel(cols, d, keep_ref, can_ref, proj_ref, uup_hbm, bup_ref, ulo_hbm, blo_ref, out_ref,
                  hid, act, ts, acc, inter, uup, ulo, upsem, losem):
    upc = [pltpu.make_async_copy(uup_hbm.at[i], uup.at[i], upsem.at[i]) for i in range(9)]
    loc = [pltpu.make_async_copy(ulo_hbm.at[i], ulo.at[i], losem.at[i]) for i in range(16)]
    for i in (3, 4, 5, 6, 7, 8, 0, 1, 2):
        upc[i].start()
    for c in loc:
        c.start()
    body = pl.ds(PAD, cols)
    prev = pl.ds(PAD - 1, cols)
    nxt = pl.ds(PAD + 1, cols)
    zero8 = jnp.zeros((4, PAD, d), F32)
    hid[:, 0:PAD, :] = zero8
    hid[:, PAD + cols:, :] = zero8
    zact = jnp.zeros((6, 2, PAD, d), F32)
    act[:, :, 0:PAD, :] = zact
    act[:, :, PAD + cols:, :] = zact
    for i in range(4):
        v = dot(can_ref[i], proj_ref[...]).astype(BF).astype(F32)
        hid[i, body, :] = v

    def three(load):
        mid = load(body)
        return [(load(prev) - mid).astype(BF), mid.astype(BF), (load(nxt) - mid).astype(BF)]

    def both(x, p):
        s = dot(x[1], uup[3 * p + 1])
        return s + dot(x[0], uup[3 * p]), s + dot(x[2], uup[3 * p + 2])

    for i in (3, 4, 5):
        upc[i].wait()
    e, o = both(three(lambda sl: hid[0, sl, :]), 1)
    ts[0, 0] = e
    ts[0, 1] = o
    for i in (6, 7, 8, 0, 1, 2):
        upc[i].wait()

    def act_row(slot, src, pair, keep):
        for par in range(2):
            v = src[par] + pair[par] + bup_ref[...]
            a = v / (1.0 + jnp.exp(-v))
            a = a.astype(BF).astype(F32)
            act[slot, par, body, :] = jnp.where(keep, a, 0.0)

    def step(k, _):
        x = three(lambda sl: hid[k + 1, sl, :] - hid[k, sl, :])
        down = both(x, 2)
        act_row(2 * k, (ts[k % 2, 0], ts[k % 2, 1]), down, (keep_ref[0] > 0) | (k > 0))
        cur = both(three(lambda sl: hid[k + 1, sl, :]), 1)
        ts[(k + 1) % 2, 0] = cur[0]
        ts[(k + 1) % 2, 1] = cur[1]
        up = both(x, 0)
        act_row(2 * k + 1, cur, (-up[0], -up[1]), (keep_ref[1] > 0) | (k < 2))
        return 0

    lax.fori_loop(0, 3, step, 0)
    for c in loc:
        c.wait()

    for t in range(2):
        h = hid[t + 1, body, :] + blo_ref[...]
        for a in range(2):
            for b in range(2):
                acc[t, a, b] = h

    def row_step(r, _):
        first = jnp.where(r == 0, 0, jnp.where(r == 2, 2, 1))
        second = jnp.where(r == 3, 3, jnp.where(r == 2, 1, 2))
        sgn = jnp.where(r == 1, 1.0, -1.0).astype(F32)
        s0 = jnp.where(r == 3, 0.0, 1.0).astype(F32)
        s1 = jnp.where(r == 0, 0.0, jnp.where(r == 1, 1.0, -1.0)).astype(F32)
        vs = [[], [], [], []]
        for t in range(2):
            def ld(par, sl):
                return act[2 * t + first, par, sl, :] + sgn * act[2 * t + second, par, sl, :]
            ev = ld(0, body)
            od = ld(1, body)
            vs[0].append((ld(1, prev) - od).astype(BF))
            vs[1].append((ev + od).astype(BF))
            vs[2].append((od - ev).astype(BF))
            vs[3].append((ev - ld(0, nxt)).astype(BF))
        m = [dot(jnp.concatenate(vs[c], axis=0), ulo[4 * r + c]) for c in range(4)]
        plus, minus = m[1] + m[2], m[1] - m[2]
        y = [plus + m[0], minus - m[3]]
        for t in range(2):
            for b in range(2):
                part = y[b][t * cols:(t + 1) * cols]
                acc[t, 0, b] += s0 * part
                acc[t, 1, b] += s1 * part
        return 0

    lax.fori_loop(0, 4, row_step, 0)
    for t in range(2):
        for a in range(2):
            for b in range(2):
                for lane in range(0, d, 128):
                    inter[lane // 128, pl.ds(b, cols, stride=2), :] = acc[t, a, b, :, lane:lane + 128]
            for lane in range(0, d, 128):
                out_ref[2 * t + a, :, lane:lane + 128] = inter[lane // 128].astype(BF)


def decode(keep, canvas, proj, uup, bup, ulo, blo):
    cols, d = canvas.shape[1], proj.shape[1]
    return pl.pallas_call(
        functools.partial(decode_kernel, cols, d),
        out_shape=jax.ShapeDtypeStruct((4, 2 * cols, d), BF),
        in_specs=[SM, VM, VM, ANY, VM, ANY, VM],
        out_specs=VM,
        scratch_shapes=[
            pltpu.VMEM((4, cols + 2 * PAD, d), F32),
            pltpu.VMEM((6, 2, cols + 2 * PAD, d), F32),
            pltpu.VMEM((2, 2, cols, d), F32),
            pltpu.VMEM((2, 2, 2, cols, d), F32),
            pltpu.VMEM((d // 128, 2 * cols, 128), F32),
            pltpu.VMEM((9, d, d), BF),
            pltpu.VMEM((16, d, d), BF),
            pltpu.SemaphoreType.DMA((9,)),
            pltpu.SemaphoreType.DMA((16,)),
        ],
        compiler_params=pltpu.CompilerParams(vmem_limit_bytes=60 * 2**20),
        name="decode",
    )(keep, canvas, proj, uup, bup, ulo, blo)


def convolve(inputs, weight):
    return lax.conv_general_dilated(
        inputs[None],
        weight,
        (1, 1),
        "SAME",
        dimension_numbers=("NHWC", "HWIO", "NHWC"),
        preferred_element_type=F32,
    )[0]


def on_device(
    latent,
    tile_reach,
    first_weight,
    first_bias,
    second_weight,
    second_bias,
    proj_weight,
    upper_weight,
    upper_bias,
    lower_weight,
    lower_bias,
):
    chans = first_weight.shape[2]
    rows = latent.shape[0]
    cols = latent.shape[1] // chans
    m = MARGIN
    n_row = lax.axis_size("row")
    n_col = lax.axis_size("col")
    row_id = lax.axis_index("row")
    col_id = lax.axis_index("col")
    total_rows = rows * n_row
    total_cols = cols * n_col
    uup, ulo = transform_weights(upper_weight, lower_weight)
    window = halo(latent.reshape(rows, cols, chans))
    reach = tile_reach[row_id, col_id]
    glob_rows = row_id * rows - m + jnp.arange(rows + 2 * m, dtype=jnp.int32)
    glob_cols = col_id * cols - m + jnp.arange(cols + 2 * m, dtype=jnp.int32)
    rows_ok = (
        (glob_rows >= row_id * rows - reach[0])
        & (glob_rows < (row_id + 1) * rows + reach[1])
        & (glob_rows >= 0)
        & (glob_rows < total_rows)
    )
    cols_ok = (
        (glob_cols >= col_id * cols - reach[2])
        & (glob_cols < (col_id + 1) * cols + reach[3])
        & (glob_cols >= 0)
        & (glob_cols < total_cols)
    )
    mask = (rows_ok[:, None] & cols_ok[None, :])[:, :, None]
    masked = jnp.where(mask, window, 0)
    active = jnp.where(mask, jax.nn.silu(convolve(masked, first_weight) + first_bias), 0.0).astype(BF)
    output = jnp.where(
        mask, masked.astype(F32) + convolve(active, second_weight) + second_bias, 0.0
    ).astype(BF)
    wide = jnp.pad(output, ((0, 0), (SIDE - m, SIDE - m), (0, 0)))
    grid_rows = jnp.arange(n_row, dtype=jnp.int32)[:, None]
    grid_cols = jnp.arange(n_col, dtype=jnp.int32)[None, :]
    low_rows = (grid_rows * rows - tile_reach[:, :, 0])[:, :, None, None]
    high_rows = ((grid_rows + 1) * rows + tile_reach[:, :, 1])[:, :, None, None]
    low_cols = (grid_cols * cols - tile_reach[:, :, 2])[:, :, None, None]
    high_cols = ((grid_cols + 1) * cols + tile_reach[:, :, 3])[:, :, None, None]
    core_rows = (row_id * rows - 1 + jnp.arange(rows + 2, dtype=jnp.int32))[None, None, :, None]
    core_cols = (col_id * cols + jnp.arange(cols, dtype=jnp.int32))[None, None, None, :]
    inside = (
        (core_rows >= jnp.maximum(low_rows, 0))
        & (core_rows < jnp.minimum(high_rows, total_rows))
        & (core_cols >= low_cols)
        & (core_cols < high_cols)
    )
    count = jnp.sum(inside.astype(F32), axis=(0, 1))[:, :, None]
    canvas = blend(wide, count)
    keep = jnp.stack(
        [
            ((row_id > 0) | (col_id > 0)).astype(jnp.int32),
            ((row_id < n_row - 1) | (col_id < n_col - 1)).astype(jnp.int32),
        ]
    )
    return decode(keep, canvas, proj_weight, uup, upper_bias[None], ulo, lower_bias[None])


def solution(mesh):
    in_specs = (P("row", "col"), P(), P(), P(), P(), P(), P(), P(), P(), P(), P())
    out_specs = P(("row", "col"), None, None)
    return jax.shard_map(on_device, mesh=mesh, in_specs=in_specs, out_specs=out_specs, check_vma=False)
```

profile of v0, /device:TPU:1, one launch (start us, length us, event | category | flops | bytes accessed | tf_op | source)
XLA Modules:
  0.0 121.4 jit_solution(17848662710243435816)
XLA Ops:
  0.0 0.7 add_convert_fusion.keep_ref
  0.7 0.8 constant_dynamic-slice_fusion
  4.6 0.9 fusion.7
  5.8 0.7 convert_reduce_fusion
  6.5 0.9 copy.34.count_ref
  7.5 2.1 %reshape.234.core_ref = bf16[32,16,320]{2,1,0:T(8,128)(2,1)} reshape(bf16[32,5120]{1,0:T(8,128)(2,1)} %param.11) | data formatting | bytes 655360 | tf_op jit(solution)/shard_map/reshape | solution.py:399
  9.5 14.6 %halo.1 = (bf16[4,8,320]{2,1,0:T(8,128)(2,1)}, bf16[4,16,320]{2,1,0:T(8,128)(2,1)}, bf16[4,8,320]{2,1,0:T(8,128)(2,1)}, bf16[32,8,320]{2,1,0:T(8,128)(2,1)}, bf1...) custom-call(bf16[32,16,320]{2,1,0:T(8,128)(2,1)} %reshape.234.core_ref), custom_call_target="tpu_custom_call" | custom-call | tf_op jit(solution)/shard_map/halo/pallas_call | solution.py:60
  24.2 0.7 slice.50
  24.9 0.7 slice.51
  25.7 0.7 slice.54
  26.4 0.7 slice.55
  27.2 1.0 slice.52
  28.1 1.0 slice.53
  29.1 0.9 maximum_bitcast_fusion.1
  30.0 1.3 %maximum_bitcast_fusion = bf16[1,32,24,320]{3,2,1,0:T(8,128)(2,1)S(1)} fusion(bf16[32,4,320]{2,1,0:T(4,128)(2,1)S(1)} %slice.53, bf16[32,16,320]{2,1,0:T(8,128)(2,1)} %reshape.234.core_ref, bf16[32,4,320]{2,1,0:T(4,128)(2,1)S(1)} %slice.52), kind=kLoop, calls=%fused_computation.13 | loop fusion | flops 1474560 | bytes 983040 | tf_op jit(solution)/shard_map/concatenate | solution.py:77
  31.6 12.4 %fusion.5 = f32[1,40,24,320]{3,0,2,1:T(1,128)S(1)} fusion(bf16[3,3,320,320]{3,2,1,0:T(8,128)(2,1)S(1)} %copy-done, bf16[1,40,24,320]{3,2,1,0:T(8,128)(2,1)S(1)} %maximum_select_fusion.1), kind=kOutput, calls=%fused_computation.8 | convolution fusion | flops 1691648000 | bytes 3686400 | tf_op jit(solution)/shard_map/conv_general_dilated | solution.py:365
  44.5 1.2 copy-done.7
  45.7 12.6 %fusion.3 = f32[1,40,24,320]{3,0,2,1:T(1,128)S(1)} fusion(bf16[3,3,320,320]{3,2,1,0:T(8,128)(2,1)S(1)} %copy-done.7, bf16[1,40,24,320]{3,2,1,0:T(8,128)(2,1)S(1)} %select_convert_fusion), kind=kOutput, calls=%fused_computation.6 | convolution fusion | flops 1691648000 | bytes 3686400 | tf_op jit(solution)/shard_map/conv_general_dilated | solution.py:365
  58.3 1.8 %fusion.2 = bf16[40,24,320]{2,1,0:T(8,128)(2,1)S(1)} fusion(f32[1,40,24,320]{3,0,2,1:T(1,128)S(1)} %fusion.3, bf16[4,4,320]{2,1,0:T(4,128)(2,1)S(1)} %slice.55, bf16[4,16,320]{2,1,0:T(8,128)(2,1)S(1)} %copy-done.4, bf16[4,4,320]{2,1,0:T(4,128)(2,1)S(1)} %slice.54, bf16[32,4,320]{2,1,0:T(4,128)(2,1)S(1)} %slice.53, bf16[32,16,320]{2,1,0:T(8,128)(2,1)S(1)} %copy-done.2, ...), kind=kLoop, calls=%fused_computation.3 | loop fusion | flops 7372800 | bytes 2459840 | tf_op jit(solution)/shard_map/convert_element_type | solution.py:420
  60.2 1.3 %pad.4.y_ref = bf16[40,32,320]{2,1,0:T(8,128)(2,1)} pad(bf16[40,24,320]{2,1,0:T(8,128)(2,1)S(1)} %fusion.2, bf16[]{:T(256)} %constant.13.clone.1), padding=0_0x4_4x0_0 | pad | bytes 1433602 | tf_op jit(solution)/shard_map/jit(_pad)/pad | solution.py:421
  61.5 26.7 %blend.1.can_ref = bf16[4,256,320]{2,1,0:T(8,128)(2,1)} custom-call(bf16[40,32,320]{2,1,0:T(8,128)(2,1)} %pad.4.y_ref, f32[34,16,1]{2,1,0:T(8,128)} %copy.34.count_ref), custom_call_target="tpu_custom_call" | custom-call | tf_op jit(solution)/shard_map/blend/pallas_call | solution.py:171
  88.2 10.5 %weights.1 = (bf16[9,512,512]{2,1,0:T(8,128)(2,1)S(1)}, bf16[16,512,512]{2,1,0:T(8,128)(2,1)}) custom-call(bf16[3,3,512,512]{3,2,1,0:T(8,128)(2,1)} %up_ref.1, bf16[3,3,512,512]{3,2,1,0:T(8,128)(2,1)} %lo_ref.1), custom_call_target="tpu_custom_call" | custom-call | flops 47185920 | bytes 22544384 | tf_op jit(solution)/shard_map/weights/pallas_call | solution.py:224
  98.7 2.2 %copy-done.1 = bf16[9,512,512]{2,1,0:T(8,128)(2,1)} copy-done((bf16[9,512,512]{2,1,0:T(8,128)(2,1)}, bf16[9,512,512]{2,1,0:T(8,128)(2,1)S(1)}, u32[]{:S(2)}) %copy-start.1) | copy-done | bytes 4718616
  100.9 20.4 %decode.1 = bf16[4,512,512]{2,1,0:T(8,128)(2,1)} custom-call(s32[2]{0:T(128)} %add_convert_fusion.keep_ref, bf16[4,256,320]{2,1,0:T(8,128)(2,1)} %blend.1.can_ref, bf16[320,512]{1,0:T(8,128)(2,1)} %proj_ref.1, bf16[9,512,512]{2,1,0:T(8,128)(2,1)} %copy-done.1, f32[1,512]{1,0:T(1,128)} %bitcast.42, bf16[16,512,512]{2,1,0:T(8,128)(2,1)} %get-tuple-element.24.ulo_hbm, ...), custom_call_target="tpu_custom_call" | custom-call | tf_op jit(solution)/shard_map/decode/pallas_call | solution.py:343
  (30 shorter events, 1.7 us)
Async XLA Ops:
  0.0 31.6 %copy-start = (bf16[3,3,320,320]{3,2,1,0:T(8,128)(2,1)S(1)}, bf16[3,3,320,320]{3,2,1,0:T(8,128)(2,1)}, u32[]{:S(2)}) copy-start(bf16[3,3,320,320]{3,2,1,0:T(8,128)(2,1)} %param.13) | copy-start | bytes 5529604
  31.6 12.4 %copy-start.5 = (f32[320]{0:T(512)S(1)}, f32[320]{0:T(512)}, u32[]{:S(2)}) copy-start(f32[320]{0:T(512)} %param.14) | copy-start | bytes 3844
  44.1 1.6 %copy-start.7 = (bf16[3,3,320,320]{3,2,1,0:T(8,128)(2,1)S(1)}, bf16[3,3,320,320]{3,2,1,0:T(8,128)(2,1)}, u32[]{:S(2)}) copy-start(bf16[3,3,320,320]{3,2,1,0:T(8,128)(2,1)} %param.15) | copy-start | bytes 5529604
  45.7 12.6 %copy-start.2 = (bf16[32,16,320]{2,1,0:T(8,128)(2,1)S(1)}, bf16[32,16,320]{2,1,0:T(8,128)(2,1)}, u32[]{:S(2)}) copy-start(bf16[32,16,320]{2,1,0:T(8,128)(2,1)} %reshape.234.core_ref) | copy-start | bytes 983044
  45.7 12.6 %copy-start.3 = (bf16[4,16,320]{2,1,0:T(8,128)(2,1)S(1)}, bf16[4,16,320]{2,1,0:T(8,128)(2,1)}, u32[]{:S(2)}) copy-start(bf16[4,16,320]{2,1,0:T(8,128)(2,1)} %get-tuple-element.16) | copy-start | bytes 122884
  45.7 12.6 %copy-start.4 = (bf16[4,16,320]{2,1,0:T(8,128)(2,1)S(1)}, bf16[4,16,320]{2,1,0:T(8,128)(2,1)}, u32[]{:S(2)}) copy-start(bf16[4,16,320]{2,1,0:T(8,128)(2,1)} %get-tuple-element.21) | copy-start | bytes 122884
  45.7 12.6 %copy-start.6 = (f32[320]{0:T(512)S(1)}, f32[320]{0:T(512)}, u32[]{:S(2)}) copy-start(f32[320]{0:T(512)} %param.16) | copy-start | bytes 3844
  98.7 2.2 %copy-start.1 = (bf16[9,512,512]{2,1,0:T(8,128)(2,1)}, bf16[9,512,512]{2,1,0:T(8,128)(2,1)S(1)}, u32[]{:S(2)}) copy-start(bf16[9,512,512]{2,1,0:T(8,128)(2,1)S(1)} %get-tuple-element.23.uup_hbm) | copy-start | bytes 14155780
where the time goes:
time: 122 us; the launch traced here: 121 us
  Pallas kernels  72.2 us (59%)
  matrix products  25 us (20%)
  local copies, waits for them, and re-layouts  14.9 us (12%)
  other arithmetic  6.5 us (5%)
  between operations  2.83 us (2%)
    pallas_call x1, Pallas kernels, blend(): pl.pallas_call(blend_kernel, out_shape=jax.ShapeDtypeStruct((deep, n_col...  26.7 us
    conv_general_dilated x2, matrix products, convolve(): lax.conv_general_dilated(inputs[None], weight, (1, 1), 'SAME', dimension_...  25 us
    pallas_call x1, Pallas kernels, decode(): pl.pallas_call(functools.partial(decode_kernel, cols, d), out_shape=jax.S...  20.4 us
    pallas_call x1, Pallas kernels, halo(): pl.pallas_call(halo_kernel, out_shape=shapes, in_specs=[VM], out_specs=[V...  14.6 us
    pallas_call x1, Pallas kernels, transform_weights(): pl.pallas_call(weights_kernel, grid=(d // step,), in_specs=[pl.BlockSpec(...  10.5 us
    unnamed x16, local copies, waits for them, and re-layouts  3.39 us
    slice x3, local copies, waits for them, and re-layouts, halo(): got[dr, -1][:, SIDE - m:]  2.47 us
    slice x3, local copies, waits for them, and re-layouts, halo(): got[dr, 1][:, :m]  2.44 us

commit v1 on v0

--- a/solution.py
+++ b/solution.py
@@ -14,9 +14,13 @@
 BF = jnp.bfloat16
 MESH = pl.DeviceIdType.MESH
 VM = pl.BlockSpec(memory_space=pltpu.VMEM)
-ANY = pl.BlockSpec(memory_space=pl.ANY)
+HB = pl.BlockSpec(memory_space=pltpu.HBM)
 SM = pl.BlockSpec(memory_space=pltpu.SMEM)
 AROUND = [(dr, dc) for dr in (-1, 0, 1) for dc in (-1, 0, 1) if (dr, dc) != (0, 0)]
+
+
+def dot(a, b):
+    return jnp.dot(a, b, preferred_element_type=F32)
 
 
 def peer(row, col, dr, dc):
@@ -66,21 +70,211 @@
         compiler_params=pltpu.CompilerParams(collective_id=0, has_side_effects=True),
         name="halo",
     )(core)
+    return lands
+
+
+def place(reach_ref, row, col, dr, dc, rows, cols):
+    n_row, n_col = lax.axis_size("row"), lax.axis_size("col")
+    there = (row + dr >= 0) & (row + dr < n_row) & (col + dc >= 0) & (col + dc < n_col)
+    r = lax.rem(row + (dr + n_row), n_row)
+    c = lax.rem(col + (dc + n_col), n_col)
+    low_r = jnp.maximum((row + dr) * rows - reach_ref[r, c, 0], 0)
+    high_r = jnp.minimum((row + dr + 1) * rows + reach_ref[r, c, 1], rows * n_row)
+    low_c = jnp.maximum((col + dc) * cols - reach_ref[r, c, 2], 0)
+    high_c = jnp.minimum((col + dc + 1) * cols + reach_ref[r, c, 3], cols * n_col)
+    return low_r, jnp.where(there, high_r, low_r), low_c, high_c
+
+
+def tile_kernel(reach_ref, core_ref, *refs):
+    lands = refs[:8]
+    w1_hbm, b1_ref, w2_hbm, b2_ref, y_ref, x, act, ga, gb, rest, w1, w2, r1, r2, wsem = refs[8:]
+    rows, cols, ch = core_ref.shape
+    m = MARGIN
+    high, wide, span = rows + 2 * m, cols + 2 * SIDE, cols + 2 * m
+    main = ch // 128 * 128
+    left = ch - main
+    wc = [pltpu.make_async_copy(src, dst, wsem.at[n]) for n, (src, dst) in enumerate(((w1_hbm, w1), (w2_hbm, w2)))]
+    for c in wc:
+        c.start()
+    row, col = lax.axis_index("row"), lax.axis_index("col")
+    low_r, high_r, low_c, high_c = place(reach_ref, row, col, 0, 0, rows, cols)
     got = dict(zip(AROUND, lands))
-    got[0, 0] = core
-    m = MARGIN
-    bands = []
-    for dr in (-1, 0, 1):
-        bands.append(
-            jnp.concatenate([got[dr, -1][:, SIDE - m :], got[dr, 0], got[dr, 1][:, :m]], axis=1)
-        )
-    return jnp.concatenate(bands, axis=0)
-
-
-def blend_kernel(y_ref, count_ref, out_ref, *refs):
-    lands, (can, send, recv, send2, recv2, self_sem) = refs[:8], refs[8:]
-    rows, cols = count_ref.shape[:2]
+    got[0, 0] = core_ref
+    top, start = row * rows - m, col * cols - SIDE
+    cid = lax.broadcasted_iota(jnp.int32, (1, wide, ch), 1) + start
+    cols_ok = (cid >= low_c) & (cid < high_c)
+
+    def masked(value, at):
+        rid = lax.broadcasted_iota(jnp.int32, value.shape, 0) + (top + at)
+        ok = (rid >= low_r) & (rid < high_r) & cols_ok
+        return jnp.where(ok, value, 0.0)
+
+    def fill(dr, at, num, src):
+        sides = [got[dr, dc][pl.ds(src, num)].astype(F32) for dc in (-1, 0, 1)]
+        x[pl.ds(at + 1, num)] = masked(jnp.concatenate(sides, axis=1), at)
+
+    fill(-1, 0, m, 0)
+    part = 8
+
+    def fill_core(n, _):
+        fill(0, m + part * n, part, part * n)
+        return 0
+
+    lax.fori_loop(0, rows // part, fill_core, 0)
+    fill(1, m + rows, m, 0)
+    for buf in (x, act):
+        buf[0] = jnp.zeros((wide, ch), F32)
+        buf[high + 1] = jnp.zeros((wide, ch), F32)
+
+    def clear(n, _):
+        act[pl.ds(part * n + 1, part), 0:8, :] = jnp.zeros((part, 8, ch), F32)
+        act[pl.ds(part * n + 1, part), wide - 8 : wide, :] = jnp.zeros((part, 8, ch), F32)
+        return 0
+
+    lax.fori_loop(0, high // part, clear, 0)
+    base = SIDE - m
+
+    def gather(buf):
+        def pair(n, _):
+            pieces = [
+                buf[pl.ds(2 * n, 2), base + dc : base + dc + span, :].reshape(2 * span, ch) for dc in (-1, 0, 1)
+            ]
+            v = jnp.concatenate(pieces, axis=1).astype(BF)
+            ga[pl.ds(pl.multiple_of(2 * span * n, 16), 2 * span), :] = v
+            return 0
+
+        def odd(n, _):
+            pieces = [
+                buf[pl.ds(2 * n + 1, 2), base + dc : base + dc + span, :].reshape(2 * span, ch) for dc in (-1, 0, 1)
+            ]
+            v = jnp.concatenate(pieces, axis=1).astype(BF)
+            gb[pl.ds(pl.multiple_of(2 * span * n, 16), 2 * span), :] = v
+            return 0
+
+        lax.fori_loop(0, (high + 2) // 2, pair, 0)
+        lax.fori_loop(0, high // 2, odd, 0)
+
+    def narrow(w, r):
+        r[...] = jnp.concatenate([w[dr, :, main:] for dr in range(3)], axis=1)
+
+    half = high // 2
+    count = half * span
+
+    def conv(w, r, b_ref, finish):
+        for n in range(2):
+            size = (high + 2) // 2 * span
+            rest[pl.ds(n * size, size), :] = dot(ga[pl.ds(n * size, size), :], r[...])
+
+        def chunk(n, _):
+            at = pl.multiple_of(n * count, 16)
+            big = (
+                dot(ga[pl.ds(at, count), :], w[0, :, :main])
+                + dot(gb[pl.ds(at, count), :], w[1, :, :main])
+                + dot(ga[pl.ds(pl.multiple_of(at + 2 * span, 16), count), :], w[2, :, :main])
+            )
+            finish(n, 0, main, big + b_ref[:, :main])
+            small = (
+                rest[pl.ds(at, count), :left]
+                + rest[pl.ds(pl.multiple_of(at + span, 8), count), left : 2 * left]
+                + rest[pl.ds(pl.multiple_of(at + 2 * span, 8), count), 2 * left :]
+            )
+            finish(n, main, ch, small + b_ref[:, main:])
+            return 0
+
+        lax.fori_loop(0, 2, chunk, 0)
+
+    def window_mask(n, width):
+        shape = (half, span, width)
+        rid = lax.broadcasted_iota(jnp.int32, shape, 0) + (top + n * half)
+        kid = lax.broadcasted_iota(jnp.int32, shape, 1) + (start + base)
+        return (rid >= low_r) & (rid < high_r) & (kid >= low_c) & (kid < high_c)
+
+    def first(n, lo, hi, v):
+        v = (v / (1.0 + jnp.exp(-v))).reshape(half, span, hi - lo)
+        v = jnp.where(window_mask(n, hi - lo), v, 0.0)
+        act[pl.ds(n * half + 1, half), base : base + span, lo:hi] = v
+
+    def second(n, lo, hi, v):
+        here = pl.ds(n * half + 1, half)
+        v = v.reshape(half, span, hi - lo) + x[here, base : base + span, lo:hi]
+        act[here, base : base + span, lo:hi] = jnp.where(window_mask(n, hi - lo), v, 0.0)
+
+    gather(x)
+    wc[0].wait()
+    narrow(w1, r1)
+    conv(w1, r1, b1_ref, first)
+    gather(act)
+    wc[1].wait()
+    narrow(w2, r2)
+    conv(w2, r2, b2_ref, second)
+
+    def emit(n, _):
+        y_ref[pl.ds(part * n, part)] = act[pl.ds(part * n + 1, part)].astype(BF)
+        return 0
+
+    lax.fori_loop(0, high // part, emit, 0)
+
+
+def tiles(reach, core, lands, w1, b1, w2, b2):
+    rows, cols, ch = core.shape
+    high, wide, span = rows + 2 * MARGIN, cols + 2 * SIDE, cols + 2 * MARGIN
+    left = 3 * (ch % 128)
+    w1, w2 = (w.reshape(3, 3 * ch, ch) for w in (w1, w2))
+    return pl.pallas_call(
+        tile_kernel,
+        out_shape=jax.ShapeDtypeStruct((high, wide, ch), BF),
+        in_specs=[SM] + [VM] * 9 + [HB, VM, HB, VM],
+        out_specs=VM,
+        scratch_shapes=[
+            pltpu.VMEM((high + 2, wide, ch), F32),
+            pltpu.VMEM((high + 2, wide, ch), F32),
+            pltpu.VMEM(((high + 2) * span, 3 * ch), BF),
+            pltpu.VMEM((high * span, 3 * ch), BF),
+            pltpu.VMEM(((high + 2) * span, left), F32),
+            pltpu.VMEM((3, 3 * ch, ch), BF),
+            pltpu.VMEM((3, 3 * ch, ch), BF),
+            pltpu.VMEM((3 * ch, left), BF),
+            pltpu.VMEM((3 * ch, left), BF),
+            pltpu.SemaphoreType.DMA((2,)),
+        ],
+        compiler_params=pltpu.CompilerParams(vmem_limit_bytes=48 * 2**20),
+        name="tiles",
+    )(reach, core, *lands, w1, b1, w2, b2)
+
+
+def spread(g):
+    outer = 0.5 * (g[0] + g[2])
+    mid = 0.5 * g[1]
+    return [g[0], outer + mid, outer - mid, g[2]]
+
+
+def upper_forms(up, out, sl, ln):
+    cols = []
+    for b in range(3):
+        w = [up[a, b, sl, ln].astype(F32) for a in range(3)]
+        cols.append([w[0], w[0] + w[1] + w[2], w[2]])
+    for p in range(3):
+        v = [cols[0][p], cols[0][p] + cols[1][p] + cols[2][p], cols[2][p]]
+        for q in range(3):
+            out[3 * p + q, sl, ln] = v[q].astype(BF)
+
+
+def lower_forms(lo, out, sl, ln):
+    cols = [spread([lo[a, b, sl, ln].astype(F32) for a in range(3)]) for b in range(3)]
+    for r in range(4):
+        v = spread([cols[b][r] for b in range(3)])
+        for c in range(4):
+            out[4 * r + c, sl, ln] = v[c].astype(BF)
+
+
+def blend_kernel(reach_ref, y_ref, up_hbm, lo_hbm, out_ref, uo_hbm, vo_hbm, *refs):
+    lands = refs[:8]
+    can, count, up, lo, uo, vo, send, recv, send2, recv2, self_sem, wsem, usem, vsem = refs[8:]
+    rows, cols, ch = can.shape
     core = rows - 2
+    loads = [pltpu.make_async_copy(up_hbm, up, wsem.at[0]), pltpu.make_async_copy(lo_hbm, lo, wsem.at[1])]
+    for c in loads:
+        c.start()
     row, col = lax.axis_index("row"), lax.axis_index("col")
     n_col = lax.axis_size("col")
     barrier = pltpu.get_barrier_semaphore()
@@ -106,6 +300,16 @@
             )
         )
         copies[-1].start()
+    shape = count.shape
+    rid = lax.broadcasted_iota(jnp.int32, shape, 0) + (row * core - 1)
+    cid = lax.broadcasted_iota(jnp.int32, shape, 1) + col * cols
+    total = jnp.zeros(shape, F32)
+    for dr in (-1, 0, 1):
+        for dc in (-1, 0, 1):
+            low_r, high_r, low_c, high_c = place(reach_ref, row, col, dr, dc, core, cols)
+            inside = (rid >= low_r) & (rid < high_r) & (cid >= low_c) & (cid < high_c)
+            total += jnp.where(inside, 1.0, 0.0)
+    count[...] = total
     for c in copies:
         c.wait()
     got = dict(zip(AROUND, lands))
@@ -121,7 +325,7 @@
             left += got[dr, -1][...].astype(F32)
             right += got[dr, 1][...].astype(F32)
         total += jnp.concatenate([left, right], axis=1)
-        n = count_ref[here]
+        n = count[here][:, :, :1]
         can[here] = jnp.where(n > 0, total / jnp.maximum(n, 1.0), 0.0).astype(BF)
 
     put(0, edge, False)
@@ -146,6 +350,35 @@
             )
         )
         copies[-1].start()
+    for c in loads:
+        c.wait()
+    depth, width = up.shape[2:]
+    block = 64
+    stores = []
+
+    def forms(form, src, dst, dst_hbm, sem):
+        def load(n):
+            sl = pl.ds(pl.multiple_of(n * block, block), block)
+            return pltpu.make_async_copy(dst.at[:, sl], dst_hbm.at[:, sl], sem.at[n])
+
+        def body(n, _):
+            def inner(k, _):
+                sl = pl.ds(pl.multiple_of(n * block + k * 16, 16), 16)
+                for lane in range(0, width, 128):
+                    form(src, dst, sl, slice(lane, lane + 128))
+                return 0
+
+            lax.fori_loop(0, block // 16, inner, 0)
+            load(n).start()
+            return 0
+
+        lax.fori_loop(0, depth // block, body, 0)
+        stores.extend(load(n) for n in range(depth // block))
+
+    forms(upper_forms, up, uo, uo_hbm, usem)
+    forms(lower_forms, lo, vo, vo_hbm, vsem)
+    for c in stores:
+        c.wait()
     own.wait()
     for o in range(1, n_col):
         copies[o - 1].wait_send()
@@ -160,85 +393,53 @@
         ).wait_recv()
 
 
-def blend(y, count):
-    rows, cols = count.shape[:2]
+def blend(reach, y, rows, cols, upper, lower):
     ch = y.shape[2]
+    d = upper.shape[2]
     n_col = lax.axis_size("col")
+    tall = rows + 2
+    deep = rows // n_col + 2
     shapes = [
-        pltpu.VMEM((rows if dr == 0 else MARGIN + 1, cols if dc == 0 else SIDE, ch), BF) for dr, dc in AROUND
+        pltpu.VMEM((tall if dr == 0 else MARGIN + 1, cols if dc == 0 else SIDE, ch), BF) for dr, dc in AROUND
     ]
-    deep = (rows - 2) // n_col + 2
     return pl.pallas_call(
         blend_kernel,
-        out_shape=jax.ShapeDtypeStruct((deep, n_col * cols, ch), BF),
-        in_specs=[VM, VM],
-        out_specs=VM,
+        out_shape=[
+            jax.ShapeDtypeStruct((deep, n_col * cols, ch), BF),
+            jax.ShapeDtypeStruct((9, d, d), BF),
+            jax.ShapeDtypeStruct((16, d, d), BF),
+        ],
+        in_specs=[SM, VM, HB, HB],
+        out_specs=[VM, HB, HB],
         scratch_shapes=shapes
         + [
-            pltpu.VMEM((rows, cols, ch), BF),
+            pltpu.VMEM((tall, cols, ch), BF),
+            pltpu.VMEM((tall, cols, 128), F32),
+            pltpu.VMEM((3, 3, d, d), BF),
+            pltpu.VMEM((3, 3, d, d), BF),
+            pltpu.VMEM((9, d, d), BF),
+            pltpu.VMEM((16, d, d), BF),
             pltpu.SemaphoreType.DMA((8,)),
             pltpu.SemaphoreType.DMA((8,)),
             pltpu.SemaphoreType.DMA((n_col,)),
             pltpu.SemaphoreType.DMA((n_col,)),
             pltpu.SemaphoreType.DMA,
+            pltpu.SemaphoreType.DMA((2,)),
+            pltpu.SemaphoreType.DMA((d // 64,)),
+            pltpu.SemaphoreType.DMA((d // 64,)),
         ],
-        compiler_params=pltpu.CompilerParams(collective_id=1, has_side_effects=True),
+        compiler_params=pltpu.CompilerParams(
+            collective_id=1, has_side_effects=True, vmem_limit_bytes=48 * 2**20
+        ),
         name="blend",
-    )(y, count)
-
-
-def spread(g):
-    outer = 0.5 * (g[0] + g[2])
-    mid = 0.5 * g[1]
-    return [g[0], outer + mid, outer - mid, g[2]]
-
-
-def weights_kernel(up_ref, lo_ref, uo_ref, lo_out_ref):
-    rows, d = up_ref.shape[2:]
-
-    def chunk(n, _):
-        sl = pl.ds(pl.multiple_of(n * 16, 16), 16)
-        for lane in range(0, d, 128):
-            ln = slice(lane, lane + 128)
-            cols = []
-            for b in range(3):
-                w = [up_ref[a, b, sl, ln].astype(F32) for a in range(3)]
-                cols.append([w[0], w[0] + w[1] + w[2], w[2]])
-            for p in range(3):
-                v = [cols[0][p], cols[0][p] + cols[1][p] + cols[2][p], cols[2][p]]
-                for q in range(3):
-                    uo_ref[3 * p + q, sl, ln] = v[q].astype(BF)
-            cols = [spread([lo_ref[a, b, sl, ln].astype(F32) for a in range(3)]) for b in range(3)]
-            for r in range(4):
-                v = spread([cols[b][r] for b in range(3)])
-                for c in range(4):
-                    lo_out_ref[4 * r + c, sl, ln] = v[c].astype(BF)
-        return 0
-
-    lax.fori_loop(0, rows // 16, chunk, 0)
-
-
-def transform_weights(upper, lower):
-    d = upper.shape[2]
-    step = 64
-    return pl.pallas_call(
-        weights_kernel,
-        grid=(d // step,),
-        in_specs=[pl.BlockSpec((3, 3, step, d), lambda i: (0, 0, i, 0))] * 2,
-        out_specs=[pl.BlockSpec((9, step, d), lambda i: (0, i, 0)), pl.BlockSpec((16, step, d), lambda i: (0, i, 0))],
-        out_shape=[jax.ShapeDtypeStruct((9, d, d), BF), jax.ShapeDtypeStruct((16, d, d), BF)],
-        compiler_params=pltpu.CompilerParams(vmem_limit_bytes=48 * 2**20),
-        cost_estimate=pl.CostEstimate(flops=20 * 9 * d * d, bytes_accessed=2 * (18 + 25) * d * d, transcendentals=0),
-        name="weights",
-    )(upper, lower)
-
-
-def dot(a, b):
-    return jnp.dot(a, b, preferred_element_type=F32)
-
-
-def decode_kernel(cols, d, keep_ref, can_ref, proj_ref, uup_hbm, bup_ref, ulo_hbm, blo_ref, out_ref,
+    )(reach, y, upper, lower)
+
+
+def decode_kernel(cols, d, can_ref, proj_ref, uup_hbm, bup_ref, ulo_hbm, blo_ref, out_ref,
                   hid, act, ts, acc, inter, uup, ulo, upsem, losem):
+    row, col = lax.axis_index("row"), lax.axis_index("col")
+    first_dev = (row == 0) & (col == 0)
+    last_dev = (row == lax.axis_size("row") - 1) & (col == lax.axis_size("col") - 1)
     upc = [pltpu.make_async_copy(uup_hbm.at[i], uup.at[i], upsem.at[i]) for i in range(9)]
     loc = [pltpu.make_async_copy(ulo_hbm.at[i], ulo.at[i], losem.at[i]) for i in range(16)]
     for i in (3, 4, 5, 6, 7, 8, 0, 1, 2):
@@ -284,12 +485,12 @@
     def step(k, _):
         x = three(lambda sl: hid[k + 1, sl, :] - hid[k, sl, :])
         down = both(x, 2)
-        act_row(2 * k, (ts[k % 2, 0], ts[k % 2, 1]), down, (keep_ref[0] > 0) | (k > 0))
+        act_row(2 * k, (ts[k % 2, 0], ts[k % 2, 1]), down, jnp.logical_not(first_dev) | (k > 0))
         cur = both(three(lambda sl: hid[k + 1, sl, :]), 1)
         ts[(k + 1) % 2, 0] = cur[0]
         ts[(k + 1) % 2, 1] = cur[1]
         up = both(x, 0)
-        act_row(2 * k + 1, cur, (-up[0], -up[1]), (keep_ref[1] > 0) | (k < 2))
+        act_row(2 * k + 1, cur, (-up[0], -up[1]), jnp.logical_not(last_dev) | (k < 2))
         return 0
 
     lax.fori_loop(0, 3, step, 0)
@@ -338,12 +539,12 @@
                 out_ref[2 * t + a, :, lane:lane + 128] = inter[lane // 128].astype(BF)
 
 
-def decode(keep, canvas, proj, uup, bup, ulo, blo):
+def decode(canvas, proj, uup, bup, ulo, blo):
     cols, d = canvas.shape[1], proj.shape[1]
     return pl.pallas_call(
         functools.partial(decode_kernel, cols, d),
         out_shape=jax.ShapeDtypeStruct((4, 2 * cols, d), BF),
-        in_specs=[SM, VM, VM, ANY, VM, ANY, VM],
+        in_specs=[VM, VM, HB, VM, HB, VM],
         out_specs=VM,
         scratch_shapes=[
             pltpu.VMEM((4, cols + 2 * PAD, d), F32),
@@ -358,18 +559,7 @@
         ],
         compiler_params=pltpu.CompilerParams(vmem_limit_bytes=60 * 2**20),
         name="decode",
-    )(keep, canvas, proj, uup, bup, ulo, blo)
-
-
-def convolve(inputs, weight):
-    return lax.conv_general_dilated(
-        inputs[None],
-        weight,
-        (1, 1),
-        "SAME",
-        dimension_numbers=("NHWC", "HWIO", "NHWC"),
-        preferred_element_type=F32,
-    )[0]
+    )(canvas, proj, uup, bup, ulo, blo)
 
 
 def on_device(
@@ -388,60 +578,11 @@
     chans = first_weight.shape[2]
     rows = latent.shape[0]
     cols = latent.shape[1] // chans
-    m = MARGIN
-    n_row = lax.axis_size("row")
-    n_col = lax.axis_size("col")
-    row_id = lax.axis_index("row")
-    col_id = lax.axis_index("col")
-    total_rows = rows * n_row
-    total_cols = cols * n_col
-    uup, ulo = transform_weights(upper_weight, lower_weight)
-    window = halo(latent.reshape(rows, cols, chans))
-    reach = tile_reach[row_id, col_id]
-    glob_rows = row_id * rows - m + jnp.arange(rows + 2 * m, dtype=jnp.int32)
-    glob_cols = col_id * cols - m + jnp.arange(cols + 2 * m, dtype=jnp.int32)
-    rows_ok = (
-        (glob_rows >= row_id * rows - reach[0])
-        & (glob_rows < (row_id + 1) * rows + reach[1])
-        & (glob_rows >= 0)
-        & (glob_rows < total_rows)
-    )
-    cols_ok = (
-        (glob_cols >= col_id * cols - reach[2])
-        & (glob_cols < (col_id + 1) * cols + reach[3])
-        & (glob_cols >= 0)
-        & (glob_cols < total_cols)
-    )
-    mask = (rows_ok[:, None] & cols_ok[None, :])[:, :, None]
-    masked = jnp.where(mask, window, 0)
-    active = jnp.where(mask, jax.nn.silu(convolve(masked, first_weight) + first_bias), 0.0).astype(BF)
-    output = jnp.where(
-        mask, masked.astype(F32) + convolve(active, second_weight) + second_bias, 0.0
-    ).astype(BF)
-    wide = jnp.pad(output, ((0, 0), (SIDE - m, SIDE - m), (0, 0)))
-    grid_rows = jnp.arange(n_row, dtype=jnp.int32)[:, None]
-    grid_cols = jnp.arange(n_col, dtype=jnp.int32)[None, :]
-    low_rows = (grid_rows * rows - tile_reach[:, :, 0])[:, :, None, None]
-    high_rows = ((grid_rows + 1) * rows + tile_reach[:, :, 1])[:, :, None, None]
-    low_cols = (grid_cols * cols - tile_reach[:, :, 2])[:, :, None, None]
-    high_cols = ((grid_cols + 1) * cols + tile_reach[:, :, 3])[:, :, None, None]
-    core_rows = (row_id * rows - 1 + jnp.arange(rows + 2, dtype=jnp.int32))[None, None, :, None]
-    core_cols = (col_id * cols + jnp.arange(cols, dtype=jnp.int32))[None, None, None, :]
-    inside = (
-        (core_rows >= jnp.maximum(low_rows, 0))
-        & (core_rows < jnp.minimum(high_rows, total_rows))
-        & (core_cols >= low_cols)
-        & (core_cols < high_cols)
-    )
-    count = jnp.sum(inside.astype(F32), axis=(0, 1))[:, :, None]
-    canvas = blend(wide, count)
-    keep = jnp.stack(
-        [
-            ((row_id > 0) | (col_id > 0)).astype(jnp.int32),
-            ((row_id < n_row - 1) | (col_id < n_col - 1)).astype(jnp.int32),
-        ]
-    )
-    return decode(keep, canvas, proj_weight, uup, upper_bias[None], ulo, lower_bias[None])
+    core = latent.reshape(rows, cols, chans)
+    lands = halo(core)
+    y = tiles(tile_reach, core, lands, first_weight, first_bias[None], second_weight, second_bias[None])
+    canvas, uup, ulo = blend(tile_reach, y, rows, cols, upper_weight, lower_weight)
+    return decode(canvas, proj_weight, uup, upper_bias[None], ulo, lower_bias[None])
 
 
 def solution(mesh):

time: 122 us -> 92.5 us (0.76)
  matrix products: 25 us -> 0 us
  other arithmetic: 6.5 us -> 0 us
  Pallas kernels: 72.2 us -> 77.5 us
  between operations: 2.83 us -> 0.05 us
    conv_general_dilated x2 -> x0, matrix products: 25 us -> none  [convolve(): lax.conv_general_dilated(inputs[None], weight, (1, 1), 'SAME', dimension_...]
    unnamed x16 -> x23, local copies, waits for them, and re-layouts: 3.39 us -> 10.7 us
    slice x8 -> x0, local copies, waits for them, and re-layouts: 6.39 us -> none  [the longest x3 2.47 us: halo(): got[dr, -1][:, SIDE - m:]]
    pallas_call x2, Pallas kernels: 37.2 us -> 42.5 us  [the longest x1 26.5 us: blend(): pl.pallas_call(blend_kernel, out_shape=[jax.ShapeDtypeStruct((deep, n_col...]
    convert_element_type x2 -> x0, other arithmetic: 2.26 us -> none  [the longest x1 1.82 us: on_device(): output = jnp.where(mask, masked.astype(F32) + convolve(active, second_wei...]
    concatenate x2 -> x0, other arithmetic: 2.23 us -> none  [halo(): return jnp.concatenate(bands, axis=0)]
    pad x1 -> x0, local copies, waits for them, and re-layouts: 1.33 us -> none  [on_device(): wide = jnp.pad(output, ((0, 0), (SIDE - m, SIDE - m), (0, 0)))]
where the time goes in v1:
time: 92.5 us; the launch traced here: 91.8 us
  Pallas kernels  77.5 us (84%)
  local copies, waits for them, and re-layouts  14.2 us (15%)
    pallas_call x1, Pallas kernels, blend(): pl.pallas_call(blend_kernel, out_shape=[jax.ShapeDtypeStruct((deep, n_col...  26.5 us
    pallas_call x1, Pallas kernels, decode(): pl.pallas_call(functools.partial(decode_kernel, cols, d), out_shape=jax.S...  20.4 us
    pallas_call x1, Pallas kernels, tiles(): pl.pallas_call(tile_kernel, out_shape=jax.ShapeDtypeStruct((high, wide, c...  15.9 us
    pallas_call x1, Pallas kernels, halo(): pl.pallas_call(halo_kernel, out_shape=shapes, in_specs=[VM], out_specs=[V...  14.6 us
    unnamed x23, local copies, waits for them, and re-layouts  10.7 us
    reshape x1, local copies, waits for them, and re-layouts, on_device(): core = latent.reshape(rows, cols, chans)  2.06 us

profile of v1, /device:TPU:1, one launch (start us, length us, event | category | flops | bytes accessed | tf_op | source)
XLA Modules:
  0.0 91.8 jit_solution(6036533887651480028)
XLA Ops:
  0.0 0.7 broadcast_in_dim.12.refs_9_
  0.7 0.7 broadcast_in_dim.13.refs_11_
  1.4 0.8 copy.13.reach_ref
  2.2 2.1 %reshape.9.core_ref = bf16[32,16,320]{2,1,0:T(8,128)(2,1)} reshape(bf16[32,5120]{1,0:T(8,128)(2,1)} %param.11) | data formatting | bytes 655360 | tf_op jit(solution)/shard_map/reshape | solution.py:581
  4.3 14.6 %halo.1 = (bf16[4,8,320]{2,1,0:T(8,128)(2,1)}, bf16[4,16,320]{2,1,0:T(8,128)(2,1)}, bf16[4,8,320]{2,1,0:T(8,128)(2,1)}, bf16[32,8,320]{2,1,0:T(8,128)(2,1)}, bf1...) custom-call(bf16[32,16,320]{2,1,0:T(8,128)(2,1)} %reshape.9.core_ref), custom_call_target="tpu_custom_call" | custom-call | tf_op jit(solution)/shard_map/halo/pallas_call | solution.py:64
  18.9 0.0 copy-start
  18.9 1.0 %copy-done = bf16[32,16,320]{2,1,0:T(8,128)(2,1)S(1)} copy-done((bf16[32,16,320]{2,1,0:T(8,128)(2,1)S(1)}, bf16[32,16,320]{2,1,0:T(8,128)(2,1)}, u32[]{:S(2)}) %copy-start) | copy-done | bytes 327704
  19.9 0.0 copy-start.1
  19.9 1.6 %copy-done.1 = bf16[3,3,320,320]{3,2,1,0:T(8,128)(2,1)S(1)} copy-done((bf16[3,3,320,320]{3,2,1,0:T(8,128)(2,1)S(1)}, bf16[3,3,320,320]{3,2,1,0:T(8,128)(2,1)}, u32[]{:S(2)}) %copy-start.1) | copy-done | bytes 1843224
  21.5 0.0 copy-start.3
  21.5 0.9 %copy-done.3 = bf16[32,8,320]{2,1,0:T(8,128)(2,1)S(1)} copy-done((bf16[32,8,320]{2,1,0:T(8,128)(2,1)S(1)}, bf16[32,8,320]{2,1,0:T(8,128)(2,1)}, u32[]{:S(2)}) %copy-start.3) | copy-done | bytes 163864
  22.5 0.9 %copy-done.4 = bf16[32,8,320]{2,1,0:T(8,128)(2,1)S(1)} copy-done((bf16[32,8,320]{2,1,0:T(8,128)(2,1)S(1)}, bf16[32,8,320]{2,1,0:T(8,128)(2,1)}, u32[]{:S(2)}) %copy-start.4) | copy-done | bytes 163864
  23.4 0.0 copy-start.5
  23.4 0.8 copy-done.5
  24.2 0.8 copy-done.6
  25.0 0.7 copy-done.7
  25.7 0.7 copy-done.8
  26.5 0.7 copy-done.9
  27.2 0.7 copy-done.10
  27.9 15.9 %tiles.1.y_ref = bf16[40,32,320]{2,1,0:T(8,128)(2,1)S(1)} custom-call(s32[8,16,4]{2,1,0:T(8,128)S(1)} %copy.13.reach_ref, bf16[32,16,320]{2,1,0:T(8,128)(2,1)S(1)} %copy-done, bf16[4,8,320]{2,1,0:T(8,128)(2,1)S(1)} %copy-done.7, bf16[4,16,320]{2,1,0:T(8,128)(2,1)S(1)} %copy-done.5, bf16[4,8,320]{2,1,0:T(8,128)(2,1)S(1)} %copy-done.8, ...), custom_call_target="tpu_custom_call" | custom-call | tf_op jit(solution)/shard_map/tiles/pallas_call | solution.py:223
  43.9 26.5 %blend.1 = (bf16[4,256,320]{2,1,0:T(8,128)(2,1)S(1)}, bf16[9,512,512]{2,1,0:T(8,128)(2,1)}, bf16[16,512,512]{2,1,0:T(8,128)(2,1)}) custom-call(s32[8,16,4]{2,1,0:T(8,128)S(1)} %copy.13.reach_ref, bf16[40,32,320]{2,1,0:T(8,128)(2,1)S(1)} %tiles.1.y_ref, bf16[3,3,512,512]{3,2,1,0:T(8,128)(2,1)} %up_hbm.1, bf16[3,3,512,512]{3,2,1,0:T(8,128)(2,1)} %lo_hbm.1), custom_call_target="tpu_custom_call" | custom-call | tf_op jit(solution)/shard_map/blend/pallas_call | solution.py:405
  70.4 0.0 copy-start.2
  70.4 0.9 copy-done.2
  71.3 20.4 %decode.1 = bf16[4,512,512]{2,1,0:T(8,128)(2,1)} custom-call(bf16[4,256,320]{2,1,0:T(8,128)(2,1)} %copy-done.2, bf16[320,512]{1,0:T(8,128)(2,1)} %proj_ref.1, bf16[9,512,512]{2,1,0:T(8,128)(2,1)} %get-tuple-element.25.uup_hbm, f32[1,512]{1,0:T(1,128)} %bitcast.6, bf16[16,512,512]{2,1,0:T(8,128)(2,1)} %get-tuple-element.26.ulo_hbm, f32[1,512]{1,0:T(1,128)} %bitcast.7), custom_call_target="tpu_custom_call" | custom-call | tf_op jit(solution)/shard_map/decode/pallas_call | solution.py:544
  (6 shorter events, 0.0 us)
Async XLA Ops:
  18.9 1.0 %copy-start = (bf16[32,16,320]{2,1,0:T(8,128)(2,1)S(1)}, bf16[32,16,320]{2,1,0:T(8,128)(2,1)}, u32[]{:S(2)}) copy-start(bf16[32,16,320]{2,1,0:T(8,128)(2,1)} %reshape.9.core_ref) | copy-start | bytes 983044
  19.9 1.6 %copy-start.1 = (bf16[3,3,320,320]{3,2,1,0:T(8,128)(2,1)S(1)}, bf16[3,3,320,320]{3,2,1,0:T(8,128)(2,1)}, u32[]{:S(2)}) copy-start(bf16[3,3,320,320]{3,2,1,0:T(8,128)(2,1)} %param.13) | copy-start | bytes 5529604
  21.5 0.9 %copy-start.3 = (bf16[32,8,320]{2,1,0:T(8,128)(2,1)S(1)}, bf16[32,8,320]{2,1,0:T(8,128)(2,1)}, u32[]{:S(2)}) copy-start(bf16[32,8,320]{2,1,0:T(8,128)(2,1)} %get-tuple-element.19.refs_3_) | copy-start | bytes 491524
  22.5 0.9 %copy-start.4 = (bf16[32,8,320]{2,1,0:T(8,128)(2,1)S(1)}, bf16[32,8,320]{2,1,0:T(8,128)(2,1)}, u32[]{:S(2)}) copy-start(bf16[32,8,320]{2,1,0:T(8,128)(2,1)} %get-tuple-element.20.refs_4_) | copy-start | bytes 491524
  23.4 0.8 copy-start.5
  24.2 0.8 copy-start.6
  25.0 0.7 copy-start.7
  25.7 0.7 copy-start.8
  26.5 0.7 copy-start.9
  27.2 0.7 copy-start.10
  70.4 0.9 copy-start.2
